TPU v7x, 32 devices: a whole 2x2x4 slice. The times are simulated.
32 devices in a mesh: groups: 2 (over y), ctx: 4 (over z), dp: 2 (over x), tp: 2 (over core).
Axes of the slice: x: 2, y: 2, z: 4, core: 2. Of those that a mesh axis runs over, the one named last changes fastest.
Arguments:
- queries: bfloat16 [4, 1280, 2048], P(('groups', 'dp'), 'ctx', 'tp'), parts along dimension 0, may hold values from -6 to 6
- key_vectors: bfloat16 [4, 1280, 2048], P(('groups', 'dp'), 'ctx', 'tp'), parts along dimension 0, may hold values from -6 to 6
- value_vectors: bfloat16 [4, 1280, 2048], P(('groups', 'dp'), 'ctx', 'tp'), parts along dimension 0, may hold values from -6 to 6
- grad_output: bfloat16 [4, 1280, 2048], P(('groups', 'dp'), 'ctx', 'tp'), parts along dimension 0, may hold values from -6 to 6
Outputs:
- normed_out: bfloat16 [4, 1280, 2048], P(('groups', 'dp'), 'ctx', 'tp'), parts along dimension 0
- grad_queries: bfloat16 [4, 1280, 2048], P(('groups', 'dp'), 'ctx', 'tp'), parts along dimension 0
- grad_keys: bfloat16 [4, 1280, 2048], P(('groups', 'dp'), 'ctx', 'tp'), parts along dimension 0
- grad_values: bfloat16 [4, 1280, 2048], P(('groups', 'dp'), 'ctx', 'tp'), parts along dimension 0
There are 2 independent parts, one for each index of `groups`. A program takes and returns all parts, laid end to end along the dimension named above; each array names one. Nothing has to cross between parts.
All inputs are finite; a program needn't handle non-finite values.
Results may differ from a plain program's by a relative error of at most 0.0059.
Values may be sent and summed in bfloat16 or wider, within the bound.
No kernel may reach another device: no remote copies, remote signals or barrier semaphores. Data moves between devices by JAX's collectives and lax.ppermute only.
A program may use at most 64 MiB of HBM per device.

v0:
```python
import jax
import jax.numpy as jnp
from jax import lax
from jax.sharding import PartitionSpec as P

DH = 128
norm_eps = 1e-06


def shards(queries, key_vectors, value_vectors, grad_output):
    block_len = queries.shape[1]
    head_count = queries.shape[2] // DH
    query_rows = queries.reshape(block_len, head_count, DH)
    key_rows = key_vectors.reshape(block_len, head_count, DH)
    value_rows = value_vectors.reshape(block_len, head_count, DH)
    grad_rows = grad_output.reshape(block_len, head_count, DH)
    rows = lax.broadcasted_iota(jnp.int32, (block_len, block_len), 0)
    columns = lax.broadcasted_iota(jnp.int32, (block_len, block_len), 1)
    causal = (columns <= rows)[None]
    local_state = jnp.einsum(
        "shd,she->hde", key_rows, value_rows, preferred_element_type=jnp.float32
    )
    state_shape = local_state.shape
    shares = lax.all_to_all(
        local_state.reshape(1, -1), "ctx", split_axis=1, concat_axis=0, tiled=True
    )
    running = jnp.cumsum(shares, axis=0)
    earlier_shares = (running - shares).astype(jnp.bfloat16)
    earlier_low = lax.all_to_all(
        earlier_shares, "ctx", split_axis=0, concat_axis=1, tiled=True
    ).reshape(state_shape)
    raw_scores = jnp.einsum(
        "thd,shd->hts", query_rows, key_rows, preferred_element_type=jnp.float32
    )
    scores_low = jnp.where(causal, raw_scores, 0.0).astype(jnp.bfloat16)
    mixed = jnp.einsum("hts,she->the", scores_low, value_rows, preferred_element_type=jnp.float32)
    mixed = mixed + jnp.einsum(
        "thd,hde->the", query_rows, earlier_low, preferred_element_type=jnp.float32
    )
    inverse = lax.rsqrt(jnp.mean(mixed * mixed, axis=-1, keepdims=True) + norm_eps)
    normed = mixed * inverse
    grad_f = grad_rows.astype(jnp.float32)
    grad_mixed = inverse * (grad_f - normed * jnp.mean(grad_f * normed, axis=-1, keepdims=True))
    grad_low = grad_mixed.astype(jnp.bfloat16)
    grad_state = jnp.einsum(
        "thd,the->hde", query_rows, grad_low, preferred_element_type=jnp.float32
    )
    grad_shares = lax.all_to_all(
        grad_state.reshape(1, -1), "ctx", split_axis=1, concat_axis=0, tiled=True
    )
    grad_total = jnp.sum(grad_shares, axis=0, keepdims=True)
    later_shares = (grad_total - jnp.cumsum(grad_shares, axis=0)).astype(jnp.bfloat16)
    later_low = lax.all_to_all(
        later_shares, "ctx", split_axis=0, concat_axis=1, tiled=True
    ).reshape(state_shape)
    raw_grad = jnp.einsum("the,she->hts", grad_low, value_rows, preferred_element_type=jnp.float32)
    grad_scores = jnp.where(causal, raw_grad, 0.0).astype(jnp.bfloat16)
    grad_q = jnp.einsum("hts,shd->thd", grad_scores, key_rows, preferred_element_type=jnp.float32)
    grad_q = grad_q + jnp.einsum(
        "the,hde->thd", grad_low, earlier_low, preferred_element_type=jnp.float32
    )
    grad_k = jnp.einsum("hts,thd->shd", grad_scores, query_rows, preferred_element_type=jnp.float32)
    grad_k = grad_k + jnp.einsum(
        "she,hde->shd", value_rows, later_low, preferred_element_type=jnp.float32
    )
    grad_v = jnp.einsum("hts,the->she", scores_low, grad_low, preferred_element_type=jnp.float32)
    grad_v = grad_v + jnp.einsum(
        "shd,hde->she", key_rows, later_low, preferred_element_type=jnp.float32
    )
    out_shape = queries.shape
    return (
        normed.astype(jnp.bfloat16).reshape(out_shape),
        grad_q.astype(jnp.bfloat16).reshape(out_shape),
        grad_k.astype(jnp.bfloat16).reshape(out_shape),
        grad_v.astype(jnp.bfloat16).reshape(out_shape),
    )


def solution(mesh):
    placed = (
        P(("groups", "dp"), "ctx", "tp"),
        P(("groups", "dp"), "ctx", "tp"),
        P(("groups", "dp"), "ctx", "tp"),
        P(("groups", "dp"), "ctx", "tp"),
    )
    return jax.shard_map(
        shards,
        mesh=mesh,
        in_specs=placed,
        out_specs=(
            P(("groups", "dp"), "ctx", "tp"),
            P(("groups", "dp"), "ctx", "tp"),
            P(("groups", "dp"), "ctx", "tp"),
            P(("groups", "dp"), "ctx", "tp"),
        ),
        check_vma=False,
    )
```

profile of v0, /device:TPU:0, one launch (start us, length us, event | category | flops | bytes accessed | tf_op | source)
XLA Modules:
  0.0 100.5 jit_solution(13804386962089446467)
XLA Ops:
  0.6 0.0 copy-start.8
  0.6 1.3 %copy.92 = bf16[40,8,8,128]{3,2,1,0:T(8,128)(2,1)S(1)} copy(bf16[40,8,8,128]{3,1,2,0:T(8,128)(2,1)} %bitcast.73) | data formatting | bytes 1310720
  1.9 0.1 copy.93
  2.1 0.0 copy-start.9
  2.1 1.2 %fusion.13 = f32[8,128,128]{2,1,0:T(8,128)} fusion(bf16[320,8,128]{2,1,0:T(8,128)(2,1)S(1)} %bitcast.61, bf16[320,8,128]{2,1,0:T(8,128)(2,1)S(1)} %bitcast.65), kind=kOutput, calls=%fused_computation.31 | convolution fusion | flops 83886080 | bytes 1835008 | tf_op jit(solution)/shard_map/shd,she->hde/dot_general | solution.py:20
  3.3 6.3 %all-to-all-start = ((f32[1,4,32768]{2,0,1:T(1,128)}), f32[1,4,32768]{2,0,1:T(1,128)S(1)}, u32[]{:S(2)}, u32[]{:S(2)}) async-start(f32[1,4,32768]{2,0,1:T(1,128)} %bitcast.1), calls=%async_computation | async-start | bytes 1048576 | tf_op jit(solution)/shard_map/all_to_all | solution.py:24
  9.6 0.1 copy.91
  9.8 0.0 copy-start
  9.8 0.0 copy-start.10
  9.8 2.0 %select_convert_fusion.1 = bf16[8,320,320]{2,1,0:T(8,128)(2,1)} fusion(pred[320,320]{1,0:T(8,128)(4,1)S(1)} %iota_compare_fusion, bf16[320,8,128]{2,1,0:T(8,128)(2,1)S(1)} %bitcast.66, bf16[320,8,128]{2,1,0:T(8,128)(2,1)S(1)} %bitcast.69), kind=kOutput, calls=%fused_computation.5 | convolution fusion | flops 211353600 | bytes 3051520 | tf_op jit(solution)/shard_map/thd,shd->hts/dot_general | solution.py:32
  11.8 12.3 %all-to-all-done = f32[1,4,32768]{2,0,1:T(1,128)S(1)} async-done(((f32[1,4,32768]{2,0,1:T(1,128)}), f32[1,4,32768]{2,0,1:T(1,128)S(1)}, u32[]{:S(2)}, u32[]{:S(2)}) %all-to-all-start) | async-done | bytes 524320 | tf_op jit(solution)/shard_map/all_to_all | solution.py:24
  24.1 0.4 fusion
  24.5 0.5 broadcast.40
  25.0 2.3 %reduce.3 = bf16[4,32768]{1,0:T(4,128)(2,1)S(1)} reduce(bf16[4,1,32768]{2,1,0:T(2,128)(2,1)S(1)} %fusion, bf16[]{:T(256)} %broadcast.40), dimensions={1}, to_apply=%fusion.reduce_sub_computation | reduce | bytes 524290 | tf_op jit(solution)/shard_map/jit(cumsum)/reduce_window_sum | solution.py:27
  27.4 1.0 reshape.148
  28.4 3.4 %all-to-all-start.1 = ((bf16[4,2,16384]{2,1,0:T(2,128)(2,1)}), bf16[4,2,16384]{2,1,0:T(2,128)(2,1)S(1)}, u32[]{:S(2)}, u32[]{:S(2)}) async-start(bf16[4,2,16384]{2,1,0:T(2,128)(2,1)} %reshape.148), calls=%async_computation.1 | async-start | bytes 524288 | tf_op jit(solution)/shard_map/all_to_all | solution.py:29
  31.8 1.2 %convert_bitcast_fusion = f32[40,8,8,128]{3,1,2,0:T(8,128)S(1)} fusion(bf16[1,320,1024]{2,1,0:T(8,128)(2,1)} %param.7), kind=kLoop, calls=%fused_computation.19 | loop fusion | flops 327680 | bytes 1966080
  33.0 0.0 copy-start.3
  33.0 0.3 copy.94
  33.3 1.3 %copy-done.3 = bf16[8,320,320]{2,1,0:T(8,128)(2,1)S(1)} copy-done((bf16[8,320,320]{2,1,0:T(8,128)(2,1)S(1)}, bf16[8,320,320]{2,1,0:T(8,128)(2,1)}, u32[]{:S(2)}) %copy-start.3) | copy-done | bytes 1638424
  34.6 1.7 %convolution_bitcast_fusion.5 = f32[320,8,128]{2,0,1:T(8,128)} fusion(bf16[8,320,320]{2,1,0:T(8,128)(2,1)S(1)} %copy-done.3, bf16[320,8,128]{2,1,0:T(8,128)(2,1)S(1)} %bitcast.62), kind=kOutput, calls=%fused_computation.15 | convolution fusion | flops 209715200 | bytes 3604480 | tf_op jit(solution)/shard_map/hts,she->the/dot_general | solution.py:36
  36.3 3.8 %all-to-all-done.1 = bf16[4,2,16384]{2,1,0:T(2,128)(2,1)S(1)} async-done(((bf16[4,2,16384]{2,1,0:T(2,128)(2,1)}), bf16[4,2,16384]{2,1,0:T(2,128)(2,1)S(1)}, u32[]{:S(2)}, u32[]{:S(2)}) %all-to-all-start.1) | async-done | bytes 262176 | tf_op jit(solution)/shard_map/all_to_all | solution.py:29
  40.1 1.0 reshape.149
  41.1 3.4 %reduce.1 = bf16[4,32768]{1,0:T(4,128)(2,1)} reduce(bf16[4,1,32768]{2,1,0:T(2,128)(2,1)} %reshape.149, bf16[]{:T(256)} %constant.16), dimensions={1}, to_apply=%all_to_all.18.reduce_sub_computation | reduce | bytes 524290 | tf_op jit(solution)/shard_map/all_to_all | solution.py:29
  44.4 1.2 %reshape.139 = bf16[8,128,128]{2,1,0:T(8,128)(2,1)S(1)} reshape(bf16[4,32768]{1,0:T(4,128)(2,1)} %reduce.1) | data formatting | bytes 524288 | tf_op jit(solution)/shard_map/reshape | solution.py:31
  45.7 2.0 %multiply_reduce_fusion.1 = (f32[320,8]{0,1:T(8,128)S(1)}, f32[320,8,128]{2,0,1:T(8,128)S(1)}) fusion(f32[320,8,128]{2,0,1:T(8,128)} %convolution_bitcast_fusion.5, bf16[8,128,128]{2,1,0:T(8,128)(2,1)S(1)} %reshape.139, bf16[320,8,128]{2,1,0:T(8,128)(2,1)S(1)} %bitcast.70), kind=kOutput, calls=%fused_computation.22 | convolution fusion | flops 84866560 | bytes 3549184 | tf_op jit(solution)/shard_map/thd,hde->the/dot_general | solution.py:37
  47.7 0.9 multiply_reduce_fusion
  48.6 1.6 %multiply_convert_fusion = (bf16[320,8,128]{2,0,1:T(8,128)(2,1)S(1)}, bf16[320,8,128]{2,0,1:T(8,128)(2,1)}) fusion(f32[320,8,128]{2,1,0:T(8,128)S(1)} %bitcast.60, f32[320,8,128]{2,0,1:T(8,128)S(1)} %get-tuple-element.7, f32[320,8]{0,1:T(8,128)S(1)} %broadcast_multiply_fusion, f32[320,8]{0,1:T(8,128)S(1)} %add_rsqrt_fusion), kind=kLoop, calls=%fused_computation.20 | loop fusion | flops 1966080 | bytes 3952640 | tf_op jit(solution)/shard_map/convert_element_type | solution.py:44
  50.2 0.0 copy-done.1
  50.2 0.4 convolution_bitcast_fusion.6
  50.6 0.0 copy-start.11
  50.6 1.0 copy.82
  51.6 4.3 %all-to-all-start.2 = ((f32[1,4,32768]{2,0,1:T(1,128)}), f32[1,4,32768]{2,0,1:T(1,128)}, u32[]{:S(2)}, u32[]{:S(2)}) async-start(f32[1,4,32768]{2,0,1:T(1,128)} %bitcast.8), calls=%async_computation.2 | async-start | bytes 1048576 | tf_op jit(solution)/shard_map/all_to_all | solution.py:48
  56.0 0.7 select_convert_fusion
  56.7 1.3 %copy-done.5 = bf16[8,320,320]{2,1,0:T(8,128)(2,1)} copy-done((bf16[8,320,320]{2,1,0:T(8,128)(2,1)}, bf16[8,320,320]{2,1,0:T(8,128)(2,1)S(1)}, u32[]{:S(2)}) %copy-start.5) | copy-done | bytes 1638424
  57.9 0.7 convolution_bitcast_fusion.4
  58.6 9.6 %all-to-all-done.2 = f32[1,4,32768]{2,0,1:T(1,128)} async-done(((f32[1,4,32768]{2,0,1:T(1,128)}), f32[1,4,32768]{2,0,1:T(1,128)}, u32[]{:S(2)}, u32[]{:S(2)}) %all-to-all-start.2) | async-done | bytes 524320 | tf_op jit(solution)/shard_map/all_to_all | solution.py:48
  68.2 2.2 %reduce_sum.29 = f32[32768]{0:T(1024)} reduce(f32[1,4,32768]{2,0,1:T(1,128)} %all-to-all-done.2, f32[]{:T(128)} %constant.9.clone.1), dimensions={0,1}, to_apply=%region_3.4 | reduce | flops 98304 | bytes 655364 | tf_op jit(solution)/shard_map/reduce_sum | solution.py:51
  70.3 2.3 %fusion.1 = bf16[4,1,32768]{2,1,0:T(2,128)(2,1)} fusion(f32[1,4,32768]{2,0,1:T(1,128)} %all-to-all-done.2, f32[32768]{0:T(1024)} %reduce_sum.29), kind=kOutput, calls=%fused_computation.3 | output fusion | flops 655360 | bytes 917504 | tf_op jit(solution)/shard_map/jit(cumsum)/reduce_window_sum | solution.py:52
  72.6 4.0 %reduce.4 = bf16[4,32768]{1,0:T(4,128)(2,1)} reduce(bf16[4,1,32768]{2,1,0:T(2,128)(2,1)} %fusion.1, bf16[]{:T(256)} %broadcast.40), dimensions={1}, to_apply=%fusion.1.reduce_sub_computation | reduce | bytes 524290 | tf_op jit(solution)/shard_map/jit(cumsum)/reduce_window_sum | solution.py:52
  76.6 2.0 %reshape.150 = bf16[4,2,16384]{2,1,0:T(2,128)(2,1)} reshape(bf16[4,32768]{1,0:T(4,128)(2,1)} %reduce.4) | data formatting | bytes 524288
  78.6 4.0 %all-to-all-start.3 = ((bf16[4,2,16384]{2,1,0:T(2,128)(2,1)}), bf16[4,2,16384]{2,1,0:T(2,128)(2,1)}, u32[]{:S(2)}, u32[]{:S(2)}) async-start(bf16[4,2,16384]{2,1,0:T(2,128)(2,1)} %reshape.150), calls=%async_computation.3 | async-start | bytes 524288 | tf_op jit(solution)/shard_map/all_to_all | solution.py:53
  82.6 0.0 copy-start.7
  82.6 1.2 %fusion.5 = bf16[320,8,128]{2,0,1:T(8,128)(2,1)} fusion(f32[320,8,128]{2,0,1:T(8,128)S(1)} %convolution_bitcast_fusion.4, bf16[8,128,128]{2,1,0:T(8,128)(2,1)S(1)} %reshape.139, bf16[320,8,128]{2,0,1:T(8,128)(2,1)S(1)} %get-tuple-element.4), kind=kOutput, calls=%fused_computation.16 | convolution fusion | flops 84541440 | bytes 2883584 | tf_op jit(solution)/shard_map/the,hde->thd/dot_general | solution.py:59
  83.8 0.0 copy-done.7
  83.8 0.4 copy.73
  84.3 1.1 %reshape.140 = bf16[1,320,1024]{2,1,0:T(8,128)(2,1)} reshape(bf16[320,8,128]{2,1,0:T(8,128)(2,1)S(1)} %copy.73) | data formatting | bytes 1310720 | tf_op jit(solution)/shard_map/reshape | solution.py:72
  85.4 1.6 %copy.78 = bf16[320,8,128]{2,1,0:T(8,128)(2,1)S(1)} copy(bf16[320,8,128]{2,0,1:T(8,128)(2,1)} %fusion.5) | data formatting | bytes 1310720 | tf_op jit(solution)/shard_map/convert_element_type | solution.py:73
  87.0 1.1 %reshape.141 = bf16[1,320,1024]{2,1,0:T(8,128)(2,1)} reshape(bf16[320,8,128]{2,1,0:T(8,128)(2,1)S(1)} %copy.78) | data formatting | bytes 1310720 | tf_op jit(solution)/shard_map/reshape | solution.py:73
  88.1 0.0 copy-done.2
  88.1 3.4 %convolution_bitcast_fusion.2 = f32[320,8,128]{2,0,1:T(8,128)} fusion(bf16[8,320,320]{2,1,0:T(8,128)(2,1)} %copy-done.5, bf16[320,8,128]{2,1,0:T(8,128)(2,1)S(1)} %bitcast.72), kind=kOutput, calls=%fused_computation.11 | convolution fusion | flops 209715200 | bytes 3604480 | tf_op jit(solution)/shard_map/hts,thd->shd/dot_general | solution.py:62
  91.5 0.0 all-to-all-done.3
  91.5 1.2 %reshape.151 = bf16[4,1,32768]{2,1,0:T(2,128)(2,1)S(1)} reshape(bf16[4,2,16384]{2,1,0:T(2,128)(2,1)} %all-to-all-done.3) | data formatting | bytes 524288
  92.7 1.7 %reduce.2 = bf16[4,32768]{1,0:T(4,128)(2,1)S(1)} reduce(bf16[4,1,32768]{2,1,0:T(2,128)(2,1)S(1)} %reshape.151, bf16[]{:T(256)} %constant.16), dimensions={1}, to_apply=%all_to_all.41.reduce_sub_computation | reduce | bytes 524290 | tf_op jit(solution)/shard_map/all_to_all | solution.py:53
  94.4 0.3 reshape.142
  94.7 0.3 fusion.16
  95.0 1.2 %copy-done.4 = bf16[8,320,320]{2,1,0:T(8,128)(2,1)S(1)} copy-done((bf16[8,320,320]{2,1,0:T(8,128)(2,1)S(1)}, bf16[8,320,320]{2,1,0:T(8,128)(2,1)}, u32[]{:S(2)}) %copy-start.4) | copy-done | bytes 1638424
  96.2 0.8 fusion.8
  97.1 0.0 copy-start.6
  97.1 0.4 copy.88
  97.5 1.1 %reshape.144 = bf16[1,320,1024]{2,1,0:T(8,128)(2,1)} reshape(bf16[320,8,128]{2,1,0:T(8,128)(2,1)S(1)} %copy.88) | data formatting | bytes 1310720 | tf_op jit(solution)/shard_map/reshape | solution.py:75
  98.6 0.3 fusion.6
  99.0 0.4 copy.85
  99.4 1.1 %reshape.143 = bf16[1,320,1024]{2,1,0:T(8,128)(2,1)} reshape(bf16[320,8,128]{2,1,0:T(8,128)(2,1)S(1)} %copy.85) | data formatting | bytes 1310720 | tf_op jit(solution)/shard_map/reshape | solution.py:74
  (13 shorter events, 0.1 us)
Async XLA Ops:
  0.6 1.3 %copy-start.8 = (bf16[1,320,1024]{2,1,0:T(8,128)(2,1)S(1)}, bf16[1,320,1024]{2,1,0:T(8,128)(2,1)}, u32[]{:S(2)}) copy-start(bf16[1,320,1024]{2,1,0:T(8,128)(2,1)} %param.6) | copy-start | bytes 1966084
  2.1 7.6 %copy-start.9 = (bf16[1,320,1024]{2,1,0:T(8,128)(2,1)S(1)}, bf16[1,320,1024]{2,1,0:T(8,128)(2,1)}, u32[]{:S(2)}) copy-start(bf16[1,320,1024]{2,1,0:T(8,128)(2,1)} %param.4) | copy-start | bytes 1966084
  3.3 20.8 %all-to-all-start = ((f32[1,4,32768]{2,0,1:T(1,128)}), f32[1,4,32768]{2,0,1:T(1,128)S(1)}, u32[]{:S(2)}, u32[]{:S(2)}) async-start(f32[1,4,32768]{2,0,1:T(1,128)} %bitcast.1), calls=%async_computation | async-start | bytes 1048576 | tf_op jit(solution)/shard_map/all_to_all | solution.py:24
  9.8 35.9 %copy-start = (bf16[40,8,8,128]{3,2,1,0:T(8,128)(2,1)}, bf16[40,8,8,128]{3,2,1,0:T(8,128)(2,1)S(1)}, u32[]{:S(2)}) copy-start(bf16[40,8,8,128]{3,2,1,0:T(8,128)(2,1)S(1)} %copy.91) | copy-start | bytes 1966084
  9.8 2.0 %copy-start.10 = (pred[320,320]{1,0:T(8,128)(4,1)}, pred[320,320]{1,0:T(8,128)(4,1)S(1)}, u32[]{:S(2)}) copy-start(pred[320,320]{1,0:T(8,128)(4,1)S(1)} %iota_compare_fusion) | copy-start | bytes 307204
  28.4 11.8 %all-to-all-start.1 = ((bf16[4,2,16384]{2,1,0:T(2,128)(2,1)}), bf16[4,2,16384]{2,1,0:T(2,128)(2,1)S(1)}, u32[]{:S(2)}, u32[]{:S(2)}) async-start(bf16[4,2,16384]{2,1,0:T(2,128)(2,1)} %reshape.148), calls=%async_computation.1 | async-start | bytes 524288 | tf_op jit(solution)/shard_map/all_to_all | solution.py:29
  33.0 1.6 %copy-start.3 = (bf16[8,320,320]{2,1,0:T(8,128)(2,1)S(1)}, bf16[8,320,320]{2,1,0:T(8,128)(2,1)}, u32[]{:S(2)}) copy-start(bf16[8,320,320]{2,1,0:T(8,128)(2,1)} %select_convert_fusion.1) | copy-start | bytes 4915204
  48.5 1.6 %copy-start.1 = (bf16[40,8,8,128]{3,2,1,0:T(8,128)(2,1)S(1)}, bf16[40,8,8,128]{3,2,1,0:T(8,128)(2,1)}, u32[]{:S(2)}) copy-start(bf16[40,8,8,128]{3,2,1,0:T(8,128)(2,1)} %copy-done) | copy-start | bytes 1966084
  50.6 5.3 %copy-start.11 = (pred[320,320]{1,0:T(8,128)(4,1)S(1)}, pred[320,320]{1,0:T(8,128)(4,1)}, u32[]{:S(2)}) copy-start(pred[320,320]{1,0:T(8,128)(4,1)} %copy-done.10) | copy-start | bytes 307204
  51.6 16.5 %all-to-all-start.2 = ((f32[1,4,32768]{2,0,1:T(1,128)}), f32[1,4,32768]{2,0,1:T(1,128)}, u32[]{:S(2)}, u32[]{:S(2)}) async-start(f32[1,4,32768]{2,0,1:T(1,128)} %bitcast.8), calls=%async_computation.2 | async-start | bytes 1048576 | tf_op jit(solution)/shard_map/all_to_all | solution.py:48
  56.7 1.3 %copy-start.5 = (bf16[8,320,320]{2,1,0:T(8,128)(2,1)}, bf16[8,320,320]{2,1,0:T(8,128)(2,1)S(1)}, u32[]{:S(2)}) copy-start(bf16[8,320,320]{2,1,0:T(8,128)(2,1)S(1)} %select_convert_fusion) | copy-start | bytes 4915204
  78.6 12.9 %all-to-all-start.3 = ((bf16[4,2,16384]{2,1,0:T(2,128)(2,1)}), bf16[4,2,16384]{2,1,0:T(2,128)(2,1)}, u32[]{:S(2)}, u32[]{:S(2)}) async-start(bf16[4,2,16384]{2,1,0:T(2,128)(2,1)} %reshape.150), calls=%async_computation.3 | async-start | bytes 524288 | tf_op jit(solution)/shard_map/all_to_all | solution.py:53
  82.6 1.2 %copy-start.7 = (bf16[320,8,128]{2,0,1:T(8,128)(2,1)S(1)}, bf16[320,8,128]{2,0,1:T(8,128)(2,1)}, u32[]{:S(2)}) copy-start(bf16[320,8,128]{2,0,1:T(8,128)(2,1)} %get-tuple-element.5) | copy-start | bytes 1966084
  85.4 2.7 %copy-start.2 = (bf16[40,8,8,128]{3,2,1,0:T(8,128)(2,1)S(1)}, bf16[40,8,8,128]{3,2,1,0:T(8,128)(2,1)}, u32[]{:S(2)}) copy-start(bf16[40,8,8,128]{3,2,1,0:T(8,128)(2,1)} %copy-done) | copy-start | bytes 1966084
  94.7 1.5 %copy-start.4 = (bf16[8,320,320]{2,1,0:T(8,128)(2,1)S(1)}, bf16[8,320,320]{2,1,0:T(8,128)(2,1)}, u32[]{:S(2)}) copy-start(bf16[8,320,320]{2,1,0:T(8,128)(2,1)} %select_convert_fusion.1) | copy-start | bytes 4915204
  97.1 1.6 %copy-start.6 = (f32[320,8,128]{2,0,1:T(8,128)S(1)}, f32[320,8,128]{2,0,1:T(8,128)}, u32[]{:S(2)}) copy-start(f32[320,8,128]{2,0,1:T(8,128)} %convolution_bitcast_fusion.2) | copy-start | bytes 3932164
where the time goes:
time: 101 us
  waiting for transfers between devices  25.7 us (25%)
  local copies, waits for them, and re-layouts  21 us (21%)
  other arithmetic  19.9 us (20%)
  starting transfers between devices  18.1 us (18%)
  matrix products  14.8 us (15%)
    all_to_all x1, waiting for transfers between devices, shards(): lax.all_to_all(local_state.reshape(1, -1), 'ctx', split_axis=1, concat_ax...  12.3 us
    unnamed x32, local copies, waits for them, and re-layouts  10.7 us
    all_to_all x1, waiting for transfers between devices, shards(): lax.all_to_all(grad_state.reshape(1, -1), 'ctx', split_axis=1, concat_axi...  9.56 us
    all_to_all x1, starting transfers between devices, shards(): lax.all_to_all(local_state.reshape(1, -1), 'ctx', split_axis=1, concat_ax...  6.32 us
    another operation x2, other arithmetic, shards(): jnp.cumsum(grad_shares, axis=0)  6.27 us
    all_to_all x1, starting transfers between devices, shards(): lax.all_to_all(grad_state.reshape(1, -1), 'ctx', split_axis=1, concat_axi...  4.33 us
    all_to_all x1, starting transfers between devices, shards(): lax.all_to_all(later_shares, 'ctx', split_axis=0, concat_axis=1, tiled=True)  4.04 us
    all_to_all x1, waiting for transfers between devices, shards(): lax.all_to_all(earlier_shares, 'ctx', split_axis=0, concat_axis=1, tiled=...  3.82 us
  transfers between devices with their start and end apart: 4, of which 3 were waited for; matrix products, arithmetic and copies ran while one was open for 15% of the time, Pallas kernels for 0%

commit v1 on v0

--- a/solution.py
+++ b/solution.py
@@ -1,3 +1,4 @@
+import functools
 import jax
 import jax.numpy as jnp
 from jax import lax
@@ -5,6 +6,32 @@
 
 DH = 128
 norm_eps = 1e-06
+
+
+def set_tokens(xx, dimension_no, slab_in):
+    local_out, u1 = (xx.shape[:dimension_no], xx.shape[dimension_no + 1 :])
+    return jnp.moveaxis(xx.reshape(*local_out, slab_in, -1, *u1), dimension_no, 0)
+
+
+def order_gates(obj, array_axis):
+    y1 = list(obj.shape[1:])
+    y1[array_axis] *= obj.shape[0]
+    return jnp.moveaxis(obj, 0, array_axis).reshape(y1)
+
+
+def direct_block_for(tile_in, which_axis, local_values, my_tile):
+    m_next = lax.axis_size(which_axis)
+    met_up, right_arr = (m_next, lax.axis_index(which_axis))
+    state_next = set_tokens(tile_in, local_values, met_up)
+    views = [state_next[right_arr]]
+    for kk in [*range(1, met_up)]:
+        w2 = state_next[right_arr ^ kk]
+        views.append(lax.ppermute(w2, which_axis, [(c, c ^ kk) for c in range(met_up)]))
+    state_next = jnp.stack(views, axis=0)[right_arr ^ jnp.arange(met_up)]
+    return order_gates(state_next, my_tile)
+
+
+_assign_series = functools.partial(direct_block_for, which_axis="ctx", local_values=1, my_tile=0)
 
 
 def shards(queries, key_vectors, value_vectors, grad_output):
@@ -21,9 +48,7 @@
         "shd,she->hde", key_rows, value_rows, preferred_element_type=jnp.float32
     )
     state_shape = local_state.shape
-    shares = lax.all_to_all(
-        local_state.reshape(1, -1), "ctx", split_axis=1, concat_axis=0, tiled=True
-    )
+    shares = _assign_series(local_state.reshape(1, -1))
     running = jnp.cumsum(shares, axis=0)
     earlier_shares = (running - shares).astype(jnp.bfloat16)
     earlier_low = lax.all_to_all(

time: 101 us -> 97.1 us (0.961)
  waiting for transfers between devices: 25.7 us -> 22.4 us
  local copies, waits for them, and re-layouts: 21 us -> 22.5 us
  other arithmetic: 19.9 us -> 18.5 us
    all_to_all x1 -> x0, waiting for transfers between devices: 12.3 us -> none  [shards(): lax.all_to_all(local_state.reshape(1, -1), 'ctx', split_axis=1, concat_ax...]
    ppermute x0 -> x3, waiting for transfers between devices: none -> 8.23 us  [direct_block_for(): lax.ppermute(w2, which_axis, [(c, c ^ kk) for c in range(met_up)])]
    all_to_all x1 -> x0, starting transfers between devices: 6.32 us -> none  [shards(): lax.all_to_all(local_state.reshape(1, -1), 'ctx', split_axis=1, concat_ax...]
    ppermute x0 -> x3, starting transfers between devices: none -> 5.76 us  [direct_block_for(): lax.ppermute(w2, which_axis, [(c, c ^ kk) for c in range(met_up)])]
    another operation x2 -> x1, other arithmetic: 2.72 us -> 0.75 us  [shards(): running = jnp.cumsum(shares, axis=0)]
    convert_element_type x0 -> x2, other arithmetic: none -> 1.1 us  [shards(): earlier_shares = (running - shares).astype(jnp.bfloat16)]
    unnamed x1, other arithmetic: 1.22 us -> 0.14 us
    unnamed x32 -> x34, local copies, waits for them, and re-layouts: 10.7 us -> 10.7 us
  transfers between devices with their start and end apart: 4 -> 6, of which waited for: 3 -> 4; matrix products, arithmetic and copies ran while one was open for 15% -> 15% of each run, Pallas kernels for 0% -> 0%
where the time goes in v1:
time: 97.1 us; the launch traced here: 96.3 us
  local copies, waits for them, and re-layouts  22.5 us (23%)
  waiting for transfers between devices  22.4 us (23%)
  other arithmetic  18.5 us (19%)
  starting transfers between devices  17.9 us (18%)
  matrix products  14 us (14%)
  between operations  1.02 us (1%)
    unnamed x34, local copies, waits for them, and re-layouts  10.7 us
    all_to_all x1, waiting for transfers between devices, shards(): lax.all_to_all(grad_state.reshape(1, -1), 'ctx', split_axis=1, concat_axi...  9.38 us
    ppermute x3, waiting for transfers between devices, direct_block_for(): lax.ppermute(w2, which_axis, [(c, c ^ kk) for c in range(met_up)])  8.23 us
    another operation x2, other arithmetic, shards(): jnp.cumsum(grad_shares, axis=0)  6.27 us
    ppermute x3, starting transfers between devices, direct_block_for(): lax.ppermute(w2, which_axis, [(c, c ^ kk) for c in range(met_up)])  5.76 us
    all_to_all x1, waiting for transfers between devices, shards(): lax.all_to_all(earlier_shares, 'ctx', split_axis=0, concat_axis=1, tiled=...  4.74 us
    all_to_all x1, starting transfers between devices, shards(): lax.all_to_all(grad_state.reshape(1, -1), 'ctx', split_axis=1, concat_axi...  4.33 us
    all_to_all x1, starting transfers between devices, shards(): lax.all_to_all(later_shares, 'ctx', split_axis=0, concat_axis=1, tiled=True)  4.04 us
  transfers between devices with their start and end apart: 6, of which 4 were waited for; matrix products, arithmetic and copies ran while one was open for 15% of the time, Pallas kernels for 0%

profile of v1, /device:TPU:0, one launch (start us, length us, event | category | flops | bytes accessed | tf_op | source)
XLA Modules:
  0.0 96.3 jit_solution(16666794008604194364)
XLA Ops:
  0.7 1.3 %copy.92 = bf16[40,8,8,128]{3,2,1,0:T(8,128)(2,1)S(1)} copy(bf16[40,8,8,128]{3,1,2,0:T(8,128)(2,1)} %bitcast.85) | data formatting | bytes 1310720
  1.9 0.1 copy.93
  2.1 0.4 fusion.11
  2.5 0.0 copy-start.9
  2.5 0.2 transpose_reshape_reshape.3
  2.8 0.5 constant_dynamic-slice_fusion
  3.2 5.1 %collective-permute-start.2 = (f32[1,32768]{1,0:T(1,128)S(1)}, f32[1,32768]{1,0:T(1,128)S(1)}, u32[]{:S(2)}, u32[]{:S(2)}) collective-permute-start(f32[1,32768]{1,0:T(1,128)S(1)} %get-tuple-element.7), channel_id=1, source_target_pairs={{0,12},{4,8},{8,4},{12,0},{1,13},{5,9},{9,5},{13,1},{2,14},{6,10},... | collective-permute-start | bytes 393224 | tf_op jit(solution)/shard_map/ppermute | solution.py:29
  8.4 0.6 collective-permute-start
  9.0 0.0 copy-start.11
  9.1 0.1 copy.91
  9.2 2.0 %select_convert_fusion.1 = bf16[8,320,320]{2,1,0:T(8,128)(2,1)} fusion(pred[320,320]{1,0:T(8,128)(4,1)S(1)} %iota_compare_fusion, bf16[320,8,128]{2,1,0:T(8,128)(2,1)S(1)} %bitcast.77, bf16[320,8,128]{2,1,0:T(8,128)(2,1)S(1)} %bitcast.80), kind=kOutput, calls=%fused_computation.4 | convolution fusion | flops 211353600 | bytes 3051520 | tf_op jit(solution)/shard_map/thd,shd->hts/dot_general | solution.py:57
  11.2 1.6 %collective-permute-done.2 = f32[1,32768]{1,0:T(1,128)S(1)} collective-permute-done((f32[1,32768]{1,0:T(1,128)S(1)}, f32[1,32768]{1,0:T(1,128)S(1)}, u32[]{:S(2)}, u32[]{:S(2)}) %collective-permute-start.2) | collective-permute-done | bytes 131104 | tf_op jit(solution)/shard_map/ppermute | solution.py:29
  12.8 6.6 %collective-permute-done.1 = f32[1,32768]{1,0:T(1,128)S(1)} collective-permute-done((f32[1,32768]{1,0:T(1,128)S(1)}, f32[1,32768]{1,0:T(1,128)S(1)}, u32[]{:S(2)}, u32[]{:S(2)}) %collective-permute-start.1) | collective-permute-done | bytes 131104 | tf_op jit(solution)/shard_map/ppermute | solution.py:29
  19.4 0.5 maximum_bitcast_fusion
  19.9 0.8 gather_fusion
  20.7 0.7 reduce_window_sum.19
  21.5 0.1 subtract_convert_fusion
  21.6 0.0 copy-start.10
  21.7 0.5 broadcast.75
  22.2 1.0 %reduce.3 = bf16[4,32768]{1,0:T(4,128)(2,1)S(1)} reduce(bf16[4,1,32768]{2,0,1:T(4,128)(2,1)S(1)} %subtract_convert_fusion, bf16[]{:T(256)} %broadcast.75), dimensions={1}, to_apply=%copy.71.reduce_sub_computation | reduce | bytes 524290 | tf_op jit(solution)/shard_map/convert_element_type | solution.py:53
  23.1 1.0 %reshape.163 = bf16[4,2,16384]{2,1,0:T(2,128)(2,1)} reshape(bf16[4,32768]{1,0:T(4,128)(2,1)S(1)} %reduce.3) | data formatting | bytes 524288
  24.1 3.7 %all-to-all-start = ((bf16[4,2,16384]{2,1,0:T(2,128)(2,1)}), bf16[4,2,16384]{2,1,0:T(2,128)(2,1)S(1)}, u32[]{:S(2)}, u32[]{:S(2)}) async-start(bf16[4,2,16384]{2,1,0:T(2,128)(2,1)} %reshape.163), calls=%async_computation | async-start | bytes 524288 | tf_op jit(solution)/shard_map/all_to_all | solution.py:54
  27.9 0.1 convert_bitcast_fusion
  28.1 0.3 copy.94
  28.3 1.3 %copy-done.3 = bf16[8,320,320]{2,1,0:T(8,128)(2,1)S(1)} copy-done((bf16[8,320,320]{2,1,0:T(8,128)(2,1)S(1)}, bf16[8,320,320]{2,1,0:T(8,128)(2,1)}, u32[]{:S(2)}) %copy-start.3) | copy-done | bytes 1638424
  29.6 1.7 %convolution_bitcast_fusion.5 = f32[320,8,128]{2,0,1:T(8,128)} fusion(bf16[8,320,320]{2,1,0:T(8,128)(2,1)S(1)} %copy-done.3, bf16[320,8,128]{2,1,0:T(8,128)(2,1)S(1)} %bitcast.73), kind=kOutput, calls=%fused_computation.14 | convolution fusion | flops 209715200 | bytes 3604480 | tf_op jit(solution)/shard_map/hts,she->the/dot_general | solution.py:61
  31.3 4.7 %all-to-all-done = bf16[4,2,16384]{2,1,0:T(2,128)(2,1)S(1)} async-done(((bf16[4,2,16384]{2,1,0:T(2,128)(2,1)}), bf16[4,2,16384]{2,1,0:T(2,128)(2,1)S(1)}, u32[]{:S(2)}, u32[]{:S(2)}) %all-to-all-start) | async-done | bytes 262176 | tf_op jit(solution)/shard_map/all_to_all | solution.py:54
  36.1 1.0 reshape.164
  37.0 3.4 %reduce.1 = bf16[4,32768]{1,0:T(4,128)(2,1)} reduce(bf16[4,1,32768]{2,1,0:T(2,128)(2,1)} %reshape.164, bf16[]{:T(256)} %constant.33), dimensions={1}, to_apply=%all_to_all.11.reduce_sub_computation | reduce | bytes 524290 | tf_op jit(solution)/shard_map/all_to_all | solution.py:54
  40.4 1.2 %reshape.144 = bf16[8,128,128]{2,1,0:T(8,128)(2,1)S(1)} reshape(bf16[4,32768]{1,0:T(4,128)(2,1)} %reduce.1) | data formatting | bytes 524288 | tf_op jit(solution)/shard_map/reshape | solution.py:56
  41.6 2.0 %multiply_reduce_fusion.1 = (f32[320,8]{0,1:T(8,128)S(1)}, f32[320,8,128]{2,0,1:T(8,128)S(1)}) fusion(f32[320,8,128]{2,0,1:T(8,128)} %convolution_bitcast_fusion.5, bf16[8,128,128]{2,1,0:T(8,128)(2,1)S(1)} %reshape.144, bf16[320,8,128]{2,1,0:T(8,128)(2,1)S(1)} %bitcast.81), kind=kOutput, calls=%fused_computation.21 | convolution fusion | flops 84866560 | bytes 3549184 | tf_op jit(solution)/shard_map/thd,hde->the/dot_general | solution.py:62
  43.6 0.9 multiply_reduce_fusion
  44.5 1.6 %multiply_convert_fusion = (bf16[320,8,128]{2,0,1:T(8,128)(2,1)S(1)}, bf16[320,8,128]{2,0,1:T(8,128)(2,1)}) fusion(f32[320,8,128]{2,1,0:T(8,128)S(1)} %bitcast.71, f32[320,8,128]{2,0,1:T(8,128)S(1)} %get-tuple-element.11, f32[320,8]{0,1:T(8,128)S(1)} %broadcast_multiply_fusion, f32[320,8]{0,1:T(8,128)S(1)} %add_rsqrt_fusion), kind=kLoop, calls=%fused_computation.19 | loop fusion | flops 1966080 | bytes 3952640 | tf_op jit(solution)/shard_map/convert_element_type | solution.py:69
  46.1 0.4 convolution_bitcast_fusion.6
  46.6 0.0 copy-start.12
  46.6 1.0 %copy.82 = f32[8,128,128]{2,1,0:T(8,128)} copy(f32[8,128,128]{1,2,0:T(8,128)S(1)} %convolution_bitcast_fusion.6) | data formatting | bytes 1048576 | tf_op jit(solution)/shard_map/thd,the->hde/dot_general | solution.py:70
  47.6 4.3 %all-to-all-start.1 = ((f32[1,4,32768]{2,0,1:T(1,128)}), f32[1,4,32768]{2,0,1:T(1,128)}, u32[]{:S(2)}, u32[]{:S(2)}) async-start(f32[1,4,32768]{2,0,1:T(1,128)} %bitcast.15), calls=%async_computation.1 | async-start | bytes 1048576 | tf_op jit(solution)/shard_map/all_to_all | solution.py:73
  51.9 0.7 select_convert_fusion
  52.6 1.3 %copy-done.5 = bf16[8,320,320]{2,1,0:T(8,128)(2,1)} copy-done((bf16[8,320,320]{2,1,0:T(8,128)(2,1)}, bf16[8,320,320]{2,1,0:T(8,128)(2,1)S(1)}, u32[]{:S(2)}) %copy-start.5) | copy-done | bytes 1638424
  53.9 0.7 convolution_bitcast_fusion.4
  54.6 9.4 %all-to-all-done.1 = f32[1,4,32768]{2,0,1:T(1,128)} async-done(((f32[1,4,32768]{2,0,1:T(1,128)}), f32[1,4,32768]{2,0,1:T(1,128)}, u32[]{:S(2)}, u32[]{:S(2)}) %all-to-all-start.1) | async-done | bytes 524320 | tf_op jit(solution)/shard_map/all_to_all | solution.py:73
  64.0 2.2 %reduce_sum.29 = f32[32768]{0:T(1024)} reduce(f32[1,4,32768]{2,0,1:T(1,128)} %all-to-all-done.1, f32[]{:T(128)} %constant.10.clone.1), dimensions={0,1}, to_apply=%region_3.4 | reduce | flops 98304 | bytes 655364 | tf_op jit(solution)/shard_map/reduce_sum | solution.py:76
  66.1 2.3 %fusion = bf16[4,1,32768]{2,1,0:T(2,128)(2,1)} fusion(f32[1,4,32768]{2,0,1:T(1,128)} %all-to-all-done.1, f32[32768]{0:T(1024)} %reduce_sum.29), kind=kOutput, calls=%fused_computation.2 | output fusion | flops 655360 | bytes 917504 | tf_op jit(solution)/shard_map/jit(cumsum)/reduce_window_sum | solution.py:77
  68.4 4.0 %reduce.4 = bf16[4,32768]{1,0:T(4,128)(2,1)} reduce(bf16[4,1,32768]{2,1,0:T(2,128)(2,1)} %fusion, bf16[]{:T(256)} %broadcast.75), dimensions={1}, to_apply=%fusion.reduce_sub_computation | reduce | bytes 524290 | tf_op jit(solution)/shard_map/jit(cumsum)/reduce_window_sum | solution.py:77
  72.4 2.0 %reshape.165 = bf16[4,2,16384]{2,1,0:T(2,128)(2,1)} reshape(bf16[4,32768]{1,0:T(4,128)(2,1)} %reduce.4) | data formatting | bytes 524288
  74.4 4.0 %all-to-all-start.2 = ((bf16[4,2,16384]{2,1,0:T(2,128)(2,1)}), bf16[4,2,16384]{2,1,0:T(2,128)(2,1)}, u32[]{:S(2)}, u32[]{:S(2)}) async-start(bf16[4,2,16384]{2,1,0:T(2,128)(2,1)} %reshape.165), calls=%async_computation.2 | async-start | bytes 524288 | tf_op jit(solution)/shard_map/all_to_all | solution.py:78
  78.4 0.0 copy-start.7
  78.4 1.2 %fusion.4 = bf16[320,8,128]{2,0,1:T(8,128)(2,1)} fusion(f32[320,8,128]{2,0,1:T(8,128)S(1)} %convolution_bitcast_fusion.4, bf16[8,128,128]{2,1,0:T(8,128)(2,1)S(1)} %reshape.144, bf16[320,8,128]{2,0,1:T(8,128)(2,1)S(1)} %get-tuple-element.4), kind=kOutput, calls=%fused_computation.15 | convolution fusion | flops 84541440 | bytes 2883584 | tf_op jit(solution)/shard_map/the,hde->thd/dot_general | solution.py:84
  79.6 0.4 copy.73
  80.0 1.1 %reshape.145 = bf16[1,320,1024]{2,1,0:T(8,128)(2,1)} reshape(bf16[320,8,128]{2,1,0:T(8,128)(2,1)S(1)} %copy.73) | data formatting | bytes 1310720 | tf_op jit(solution)/shard_map/reshape | solution.py:97
  81.2 1.6 %copy.78 = bf16[320,8,128]{2,1,0:T(8,128)(2,1)S(1)} copy(bf16[320,8,128]{2,0,1:T(8,128)(2,1)} %fusion.4) | data formatting | bytes 1310720 | tf_op jit(solution)/shard_map/convert_element_type | solution.py:98
  82.7 1.1 %reshape.146 = bf16[1,320,1024]{2,1,0:T(8,128)(2,1)} reshape(bf16[320,8,128]{2,1,0:T(8,128)(2,1)S(1)} %copy.78) | data formatting | bytes 1310720 | tf_op jit(solution)/shard_map/reshape | solution.py:98
  83.9 3.4 %convolution_bitcast_fusion.2 = f32[320,8,128]{2,0,1:T(8,128)} fusion(bf16[8,320,320]{2,1,0:T(8,128)(2,1)} %copy-done.5, bf16[320,8,128]{2,1,0:T(8,128)(2,1)S(1)} %bitcast.83), kind=kOutput, calls=%fused_computation.10 | convolution fusion | flops 209715200 | bytes 3604480 | tf_op jit(solution)/shard_map/hts,thd->shd/dot_general | solution.py:87
  87.3 1.2 %reshape.166 = bf16[4,1,32768]{2,1,0:T(2,128)(2,1)S(1)} reshape(bf16[4,2,16384]{2,1,0:T(2,128)(2,1)} %all-to-all-done.2) | data formatting | bytes 524288
  88.5 1.7 %reduce.2 = bf16[4,32768]{1,0:T(4,128)(2,1)S(1)} reduce(bf16[4,1,32768]{2,1,0:T(2,128)(2,1)S(1)} %reshape.166, bf16[]{:T(256)} %constant.33), dimensions={1}, to_apply=%all_to_all.14.reduce_sub_computation | reduce | bytes 524290 | tf_op jit(solution)/shard_map/all_to_all | solution.py:78
  90.2 0.3 reshape.147
  90.5 0.3 fusion.14
  90.8 1.2 %copy-done.4 = bf16[8,320,320]{2,1,0:T(8,128)(2,1)S(1)} copy-done((bf16[8,320,320]{2,1,0:T(8,128)(2,1)S(1)}, bf16[8,320,320]{2,1,0:T(8,128)(2,1)}, u32[]{:S(2)}) %copy-start.4) | copy-done | bytes 1638424
  92.0 0.8 fusion.7
  92.8 0.4 copy.88
  93.3 1.1 %reshape.149 = bf16[1,320,1024]{2,1,0:T(8,128)(2,1)} reshape(bf16[320,8,128]{2,1,0:T(8,128)(2,1)S(1)} %copy.88) | data formatting | bytes 1310720 | tf_op jit(solution)/shard_map/reshape | solution.py:100
  94.4 0.3 fusion.5
  94.7 0.4 copy.85
  95.2 1.1 %reshape.148 = bf16[1,320,1024]{2,1,0:T(8,128)(2,1)} reshape(bf16[320,8,128]{2,1,0:T(8,128)(2,1)S(1)} %copy.85) | data formatting | bytes 1310720 | tf_op jit(solution)/shard_map/reshape | solution.py:99
  (26 shorter events, 0.1 us)
Async XLA Ops:
  0.6 1.3 %copy-start.8 = (bf16[1,320,1024]{2,1,0:T(8,128)(2,1)S(1)}, bf16[1,320,1024]{2,1,0:T(8,128)(2,1)}, u32[]{:S(2)}) copy-start(bf16[1,320,1024]{2,1,0:T(8,128)(2,1)} %param.6) | copy-start | bytes 1966084
  2.5 6.5 %copy-start.9 = (bf16[1,320,1024]{2,1,0:T(8,128)(2,1)S(1)}, bf16[1,320,1024]{2,1,0:T(8,128)(2,1)}, u32[]{:S(2)}) copy-start(bf16[1,320,1024]{2,1,0:T(8,128)(2,1)} %param.4) | copy-start | bytes 1966084
  3.2 9.5 %collective-permute-start.2 = (f32[1,32768]{1,0:T(1,128)S(1)}, f32[1,32768]{1,0:T(1,128)S(1)}, u32[]{:S(2)}, u32[]{:S(2)}) collective-permute-start(f32[1,32768]{1,0:T(1,128)S(1)} %get-tuple-element.7), channel_id=1, source_target_pairs={{0,12},{4,8},{8,4},{12,0},{1,13},{5,9},{9,5},{13,1},{2,14},{6,10},... | collective-permute-start | bytes 393224 | tf_op jit(solution)/shard_map/ppermute | solution.py:29
  8.3 11.1 %collective-permute-start.1 = (f32[1,32768]{1,0:T(1,128)S(1)}, f32[1,32768]{1,0:T(1,128)S(1)}, u32[]{:S(2)}, u32[]{:S(2)}) collective-permute-start(f32[1,32768]{1,0:T(1,128)S(1)} %get-tuple-element.8), channel_id=1, source_target_pairs={{0,8},{4,12},{8,0},{12,4},{1,9},{5,13},{9,1},{13,5},{2,10},{6,14},... | collective-permute-start | bytes 393224 | tf_op jit(solution)/shard_map/ppermute | solution.py:29
  8.4 11.1 %collective-permute-start = (f32[1,32768]{1,0:T(1,128)S(1)}, f32[1,32768]{1,0:T(1,128)S(1)}, u32[]{:S(2)}, u32[]{:S(2)}) collective-permute-start(f32[1,32768]{1,0:T(1,128)S(1)} %get-tuple-element.9), channel_id=1, source_target_pairs={{0,4},{4,0},{8,12},{12,8},{1,5},{5,1},{9,13},{13,9},{2,6},{6,2},{1... | collective-permute-start | bytes 393224 | tf_op jit(solution)/shard_map/ppermute | solution.py:29
  9.0 2.1 %copy-start.11 = (pred[320,320]{1,0:T(8,128)(4,1)}, pred[320,320]{1,0:T(8,128)(4,1)S(1)}, u32[]{:S(2)}) copy-start(pred[320,320]{1,0:T(8,128)(4,1)S(1)} %iota_compare_fusion) | copy-start | bytes 307204
  9.2 32.5 %copy-start = (bf16[40,8,8,128]{3,2,1,0:T(8,128)(2,1)}, bf16[40,8,8,128]{3,2,1,0:T(8,128)(2,1)S(1)}, u32[]{:S(2)}) copy-start(bf16[40,8,8,128]{3,2,1,0:T(8,128)(2,1)S(1)} %copy.91) | copy-start | bytes 1966084
  21.6 6.3 %copy-start.10 = (bf16[1,320,1024]{2,1,0:T(8,128)(2,1)S(1)}, bf16[1,320,1024]{2,1,0:T(8,128)(2,1)}, u32[]{:S(2)}) copy-start(bf16[1,320,1024]{2,1,0:T(8,128)(2,1)} %param.7) | copy-start | bytes 1966084
  24.1 11.9 %all-to-all-start = ((bf16[4,2,16384]{2,1,0:T(2,128)(2,1)}), bf16[4,2,16384]{2,1,0:T(2,128)(2,1)S(1)}, u32[]{:S(2)}, u32[]{:S(2)}) async-start(bf16[4,2,16384]{2,1,0:T(2,128)(2,1)} %reshape.163), calls=%async_computation | async-start | bytes 524288 | tf_op jit(solution)/shard_map/all_to_all | solution.py:54
  28.0 1.6 %copy-start.3 = (bf16[8,320,320]{2,1,0:T(8,128)(2,1)S(1)}, bf16[8,320,320]{2,1,0:T(8,128)(2,1)}, u32[]{:S(2)}) copy-start(bf16[8,320,320]{2,1,0:T(8,128)(2,1)} %select_convert_fusion.1) | copy-start | bytes 4915204
  44.5 1.6 %copy-start.1 = (bf16[40,8,8,128]{3,2,1,0:T(8,128)(2,1)S(1)}, bf16[40,8,8,128]{3,2,1,0:T(8,128)(2,1)}, u32[]{:S(2)}) copy-start(bf16[40,8,8,128]{3,2,1,0:T(8,128)(2,1)} %copy-done) | copy-start | bytes 1966084
  46.6 5.3 %copy-start.12 = (pred[320,320]{1,0:T(8,128)(4,1)S(1)}, pred[320,320]{1,0:T(8,128)(4,1)}, u32[]{:S(2)}) copy-start(pred[320,320]{1,0:T(8,128)(4,1)} %copy-done.11) | copy-start | bytes 307204
  47.6 16.4 %all-to-all-start.1 = ((f32[1,4,32768]{2,0,1:T(1,128)}), f32[1,4,32768]{2,0,1:T(1,128)}, u32[]{:S(2)}, u32[]{:S(2)}) async-start(f32[1,4,32768]{2,0,1:T(1,128)} %bitcast.15), calls=%async_computation.1 | async-start | bytes 1048576 | tf_op jit(solution)/shard_map/all_to_all | solution.py:73
  52.6 1.3 %copy-start.5 = (bf16[8,320,320]{2,1,0:T(8,128)(2,1)}, bf16[8,320,320]{2,1,0:T(8,128)(2,1)S(1)}, u32[]{:S(2)}) copy-start(bf16[8,320,320]{2,1,0:T(8,128)(2,1)S(1)} %select_convert_fusion) | copy-start | bytes 4915204
  74.4 12.9 %all-to-all-start.2 = ((bf16[4,2,16384]{2,1,0:T(2,128)(2,1)}), bf16[4,2,16384]{2,1,0:T(2,128)(2,1)}, u32[]{:S(2)}, u32[]{:S(2)}) async-start(bf16[4,2,16384]{2,1,0:T(2,128)(2,1)} %reshape.165), calls=%async_computation.2 | async-start | bytes 524288 | tf_op jit(solution)/shard_map/all_to_all | solution.py:78
  78.4 1.2 %copy-start.7 = (bf16[320,8,128]{2,0,1:T(8,128)(2,1)S(1)}, bf16[320,8,128]{2,0,1:T(8,128)(2,1)}, u32[]{:S(2)}) copy-start(bf16[320,8,128]{2,0,1:T(8,128)(2,1)} %get-tuple-element.5) | copy-start | bytes 1966084
  81.2 2.7 %copy-start.2 = (bf16[40,8,8,128]{3,2,1,0:T(8,128)(2,1)S(1)}, bf16[40,8,8,128]{3,2,1,0:T(8,128)(2,1)}, u32[]{:S(2)}) copy-start(bf16[40,8,8,128]{3,2,1,0:T(8,128)(2,1)} %copy-done) | copy-start | bytes 1966084
  90.4 1.5 %copy-start.4 = (bf16[8,320,320]{2,1,0:T(8,128)(2,1)S(1)}, bf16[8,320,320]{2,1,0:T(8,128)(2,1)}, u32[]{:S(2)}) copy-start(bf16[8,320,320]{2,1,0:T(8,128)(2,1)} %select_convert_fusion.1) | copy-start | bytes 4915204
  92.8 1.6 %copy-start.6 = (f32[320,8,128]{2,0,1:T(8,128)S(1)}, f32[320,8,128]{2,0,1:T(8,128)}, u32[]{:S(2)}) copy-start(f32[320,8,128]{2,0,1:T(8,128)} %convolution_bitcast_fusion.2) | copy-start | bytes 3932164
